TPU v7x, 512 devices: a whole 4x4x16 slice. The times are simulated.
512 devices in a mesh: member: 16 (over x, z_hi), slab: 32 (over y, z_lo, core).
Axes of the slice: x: 4, y: 4, z: 16 (z_hi: 4, z_lo: 4; z = z_hi * 4 + z_lo), core: 2. Of those that a mesh axis runs over, the one named last changes fastest.
Arguments:
- fluid_head_start: float32 [192, 512, 128], P('member', 'slab'), may hold values from -6 to 6
- conductivity_matrix: float32 [192, 512, 128], P('member', 'slab'), may hold values from 0.1 to 1
- well_rates: float32 [512, 128], P('slab'), may hold values from -3 to 3
- cell_layer: int32 [512, 128], P('slab'), may hold values from 0 to 7
- pixel_coords: int32 [2, 4096], replicated, may hold values from 0 to 63
- obs_index: int32 [1024], replicated, may hold values from 0 to 4095
- obs_value: float32 [1024], replicated, may hold values from -0.6 to 0.6
- obs_sigma: float32 [1024], replicated, may hold values from 0.05 to 0.5
Outputs:
- analysed: float32 [192, 512, 128], P('member', 'slab')
- subsidence: float32 [4096, 192], P(('member', 'slab'))
All inputs are finite; a program needn't handle non-finite values.
Results may differ from a plain program's by a relative error of at most 0.00028.
Values sent between devices are 32-bit elements; how exact they have to be, the bound alone decides.
A program may use at most 64 MiB of HBM per device.

v0:
```python
import math
import jax
import jax.numpy as jnp
from jax import lax
from jax.sharding import PartitionSpec as P

STEPS = 4
time_step = 0.15
pixel_span = 64.0
top_depth = 2.0


def padded(value, sides, width):
    for axis, dim in sides:
        size, length = (lax.axis_size(axis), value.shape[dim])
        up = [(i, (i + 1) % size) for i in range(size - 1)]
        down = [(j, i) for i, j in up]
        last = lax.slice_in_dim(value, length - width, length, axis=dim)
        initial = lax.slice_in_dim(value, 0, width, axis=dim)
        before = lax.ppermute(last, axis, up)
        after = lax.ppermute(initial, axis, down)
        value = jnp.concatenate([before, value, after], axis=dim)
    return value


def advance_in_time(fluid_head_grid, perm_field, source, open_faces):
    mobility = perm_field * (1.0 + 0.5 * jnp.tanh(fluid_head_grid))
    sample_vectors, height, across_cells = fluid_head_grid.shape
    across = 0.5 * (mobility[:, 1:] + mobility[:, :-1]) * open_faces[None, :, None]
    flux_rows = across * (fluid_head_grid[:, 1:] - fluid_head_grid[:, :-1])
    zero_row = jnp.zeros((sample_vectors, 1, across_cells), fluid_head_grid.dtype)
    inflow = jnp.concatenate([flux_rows, zero_row], 1) - jnp.concatenate([zero_row, flux_rows], 1)
    along = 0.5 * (mobility[:, :, 1:] + mobility[:, :, :-1])
    flux_cols = along * (fluid_head_grid[:, :, 1:] - fluid_head_grid[:, :, :-1])
    zero_col = jnp.zeros((sample_vectors, height, 1), fluid_head_grid.dtype)
    inflow = inflow + (
        jnp.concatenate([flux_cols, zero_col], 2) - jnp.concatenate([zero_col, flux_cols], 2)
    )
    return fluid_head_grid + time_step * (inflow + source[None])


def kernel_rows(pixel_x, pixel_y, cell_x, cell_y, depth, volume):
    delta_x = cell_x[None, :] - pixel_x[:, None]
    delta_y = cell_y[None, :] - pixel_y[:, None]
    radius = delta_x * delta_x + delta_y * delta_y + depth[None, :] * depth[None, :]
    return volume * depth[None, :] / (radius * jnp.sqrt(radius))


def gram_terms(predicted, obs_value, obs_sigma, owned):
    centre = jnp.mean(predicted, axis=1)
    anomaly = predicted - centre[:, None]
    inverse_var = 1.0 / (obs_sigma * obs_sigma)
    weighted = anomaly * inverse_var[:, None]
    gram = lax.dot_general(
        anomaly, weighted, (((0,), (0,)), ((), ())), precision=lax.Precision.HIGHEST
    )
    rhs = jnp.dot(owned * (obs_value - centre), weighted, precision=lax.Precision.HIGHEST)
    return (gram, rhs)


def finish(gram, rhs, sample_vector_pile):
    sample_vectors = sample_vector_pile.shape[0]
    ident = jnp.eye(sample_vectors, dtype=gram.dtype)
    gram = gram + (sample_vectors - 1.0) * ident
    factor = jnp.linalg.cholesky(gram)
    inverse = jax.scipy.linalg.solve_triangular(factor, ident, lower=True)
    weights = jnp.dot(
        inverse.T,
        jnp.dot(inverse, rhs, precision=lax.Precision.HIGHEST),
        precision=lax.Precision.HIGHEST,
    )
    transform = jnp.sqrt(sample_vectors - 1.0) * inverse.T
    mix = weights[:, None] + transform
    centre = jnp.mean(sample_vector_pile, axis=0)
    spread = sample_vector_pile - centre[None]
    return centre[None] + lax.dot_general(
        mix, spread, (((0,), (0,)), ((), ())), precision=lax.Precision.HIGHEST
    )


def face_mask(first_global, height, total_rows):
    index = first_global + jnp.arange(height - 1, dtype=jnp.int32)
    return ((index >= 0) & (index + 1 <= total_rows - 1)).astype(jnp.float32)


def shards(
    fluid_head_start,
    conductivity_matrix,
    well_rates,
    cell_layer,
    pixel_coords,
    obs_index,
    obs_value,
    obs_sigma,
):
    local_members, slab_rows, across_cells = fluid_head_start.shape
    member_count = lax.axis_size("member")
    slab_count = lax.axis_size("slab")
    slab_index = lax.axis_index("slab")
    member_index = lax.axis_index("member")
    total_rows = slab_rows * slab_count
    rim_width = STEPS
    static = jnp.concatenate([conductivity_matrix, well_rates[None]], 0)
    static_ext = padded(static, (("slab", 1),), rim_width)
    permeability_extended = static_ext[:-1]
    source_extended = static_ext[-1]
    fluid_head_grid = padded(fluid_head_start, (("slab", 1),), STEPS)
    open_faces = face_mask(slab_index * slab_rows - STEPS, slab_rows + 2 * STEPS, total_rows)
    for repeat in range(STEPS):
        fluid_head_grid = advance_in_time(
            fluid_head_grid, permeability_extended, source_extended, open_faces
        )
    predicted_ensemble = fluid_head_grid[:, STEPS : STEPS + slab_rows]
    collected_states = lax.all_to_all(
        predicted_ensemble, "member", split_axis=1, concat_axis=0, tiled=True
    )
    sample_vectors = collected_states.shape[0]
    sub_rows = collected_states.shape[1]
    sample_vector_pile = collected_states.reshape(sample_vectors, sub_rows * across_cells)
    row_global = (
        slab_index * slab_rows + member_index * sub_rows + jnp.arange(sub_rows, dtype=jnp.int32)
    )
    row_pos = (row_global.astype(jnp.float32) + 0.5) * (pixel_span / total_rows)
    col_pos = (jnp.arange(across_cells).astype(jnp.float32) + 0.5) * (pixel_span / across_cells)
    cell_x = jnp.broadcast_to(row_pos[:, None], (sub_rows, across_cells)).reshape(-1)
    cell_y = col_pos[None, :].reshape(-1)
    layers = lax.dynamic_slice_in_dim(cell_layer, member_index * sub_rows, sub_rows, 0).astype(
        jnp.float32
    )
    depth = (top_depth + layers).reshape(-1)
    volume = pixel_span * pixel_span / (total_rows * across_cells)
    pixel_f = pixel_coords.astype(jnp.float32)
    pixel_total = pixel_coords.shape[1]
    own_rows = pixel_total // (member_count * slab_count)
    own_first = lax.axis_index(("member", "slab")) * own_rows
    block = math.gcd(pixel_total, 512)

    def pixel_block(offset):
        coords = lax.dynamic_slice_in_dim(pixel_f, offset, block, 1)
        kern = kernel_rows(coords[0], coords[1], cell_x, cell_y, depth, volume)
        return lax.dot_general(
            kern, sample_vector_pile, (((1,), (1,)), ((), ())), precision=lax.Precision.HIGHEST
        )

    offsets = 0 + block * jnp.arange(pixel_total // block, dtype=jnp.int32)
    whole = lax.psum(
        lax.map(pixel_block, offsets).reshape(pixel_total, sample_vectors), ("member", "slab")
    )
    own_part = lax.dynamic_slice_in_dim(whole, own_first, own_rows, 0)
    predicted = jnp.take(whole, obs_index, axis=0)
    gram, rhs = gram_terms(predicted, obs_value, obs_sigma, jnp.ones_like(obs_value))
    analysed = finish(gram, rhs, sample_vector_pile).reshape(sample_vectors, sub_rows, across_cells)
    returned = lax.all_to_all(analysed, "member", split_axis=0, concat_axis=1, tiled=True)
    return (returned, own_part)


def solution(mesh):
    return jax.shard_map(
        shards,
        mesh=mesh,
        in_specs=(
            P("member", "slab", None),
            P("member", "slab", None),
            P("slab", None),
            P("slab", None),
            P(),
            P(),
            P(),
            P(),
        ),
        out_specs=(P("member", "slab", None), P(("member", "slab"), None)),
        check_vma=False,
    )
```

profile of v0, /device:TPU:8, one launch (start us, length us, event | category | flops | bytes accessed | tf_op | source)
XLA Modules:
  0.0 677.4 jit_solution(5419804613752783939)
XLA Ops:
  7.2 0.8 fusion.83
  8.0 1.9 collective-permute-start
  10.0 6.3 collective-permute-start.1
  16.3 0.9 copy.28
  17.9 1.9 collective-permute-start.2
  19.9 6.3 collective-permute-start.3
  26.3 0.9 copy_dynamic-update-slice_fusion
  30.9 0.8 slice_add_fusion.8
  31.6 17.7 %all-to-all-start = ((f32[12,16,128]{2,0,1:T(8,128)}), f32[12,16,128]{2,0,1:T(8,128)S(1)}, u32[]{:S(2)}, u32[]{:S(2)}) async-start(f32[12,16,128]{2,0,1:T(8,128)} %slice_add_fusion.8), calls=%async_computation | async-start | bytes 262144 | tf_op jit(solution)/shard_map/all_to_all | solution.py:114
  50.1 15.0 %all-to-all-done = f32[12,16,128]{2,0,1:T(8,128)S(1)} async-done(((f32[12,16,128]{2,0,1:T(8,128)}), f32[12,16,128]{2,0,1:T(8,128)S(1)}, u32[]{:S(2)}, u32[]{:S(2)}) %all-to-all-start) | async-done | bytes 98336 | tf_op jit(solution)/shard_map/all_to_all | solution.py:114
  65.1 24.8 %while.14 = (s32[]{:T(128)}, f32[8,512,192]{1,2,0:T(8,128)S(1)}, f32[1,128]{1,0:T(1,128)S(1)}, f32[1,1]{1,0:T(1,128)}, s32[8]{0:T(128)S(1)}, /*index=5*/f32[2,40...) while((s32[]{:T(128)}, f32[8,512,192]{1,2,0:T(8,128)S(1)}, ...), condition=%wide.region_2.3_spmd.clone, body=%wide.region_1.2_spmd.clone.sunk | while | flops 151389696 | bytes 507079 | solution.py:147
  89.9 3.4 copy.29
  94.1 486.0 %all-reduce.21.cloned.1.call-done = f32[4096,192]{1,0:T(8,128)} async-done(((f32[4096,192]{1,0:T(8,128)}), f32[4096,192]{1,0:T(8,128)}) %all-reduce.21.cloned.1.call-update) | async-done | bytes 3145744 | tf_op jit(solution)/shard_map/psum | solution.py:146
  580.1 5.8 gather_fusion
  586.3 2.5 fusion.17
  589.0 11.7 %cholesky.50 = f32[128,128]{1,0:T(8,128)S(1)} custom-call(f32[128,128]{1,0:T(8,128)S(1)} %cholesky.121), custom_call_target="Cholesky" | custom-call | tf_op jit(solution)/shard_map/jit(cholesky)/cholesky | solution.py:65
  600.8 0.9 fusion.19
  602.3 9.8 %custom-call.15 = f32[1,128,128]{1,2,0:T(8,128)S(1)} custom-call(f32[1,128,128]{2,1,0:T(8,128)S(1)} %get-tuple-element.153), custom_call_target="InvertDiagBlocksLowerTriangular" | custom-call | tf_op jit(solution)/shard_map/jit(cholesky)/cholesky | solution.py:65
  612.5 5.8 cholesky.108
  620.4 19.9 %custom-call.16 = f32[2,128,128]{1,2,0:T(8,128)S(1)} custom-call(f32[2,128,128]{2,1,0:T(8,128)S(1)} %pad_maximum_fusion.2), custom_call_target="InvertDiagBlocksLowerTriangular" | custom-call | tf_op jit(solution)/shard_map/jit(_solve_triangular)/triangular_solve | solution.py:66
  641.7 1.4 convolution_add_fusion
  643.1 11.5 %all-to-all-start.1 = ((f32[192,1,128]{2,1,0:T(1,128)}), f32[192,1,128]{2,1,0:T(1,128)S(1)}, u32[]{:S(2)}, u32[]{:S(2)}) async-start(f32[192,1,128]{2,1,0:T(1,128)} %bitcast.21), calls=%async_computation.1 | async-start | bytes 196608 | tf_op jit(solution)/shard_map/all_to_all | solution.py:153
  654.7 1.3 constant_dynamic-slice_fusion
  656.0 13.9 %all-to-all-done.1 = f32[192,1,128]{2,1,0:T(1,128)S(1)} async-done(((f32[192,1,128]{2,1,0:T(1,128)}), f32[192,1,128]{2,1,0:T(1,128)S(1)}, u32[]{:S(2)}, u32[]{:S(2)}) %all-to-all-start.1) | async-done | bytes 98336 | tf_op jit(solution)/shard_map/all_to_all | solution.py:153
  (110 shorter events, 21.2 us)
Async XLA Ops:
  8.0 18.2 %collective-permute-start = (f32[12,4,128]{2,0,1:T(8,128)S(1)}, f32[12,4,128]{2,0,1:T(8,128)S(1)}, u32[]{:S(2)}, u32[]{:S(2)}) collective-permute-start(f32[12,4,128]{2,0,1:T(8,128)S(1)} %copy.37), channel_id=1, source_target_pairs={{0,1},{1,2},{2,3},{3,4},{4,5},{5,6},{6,7},{7,8},{8,9},{9,10},{10,1... | collective-permute-start | bytes 73736 | tf_op jit(solution)/shard_map/ppermute | solution.py:20
  10.0 17.2 %collective-permute-start.1 = (f32[12,4,128]{2,0,1:T(8,128)S(1)}, f32[12,4,128]{2,0,1:T(8,128)S(1)}, u32[]{:S(2)}, u32[]{:S(2)}) collective-permute-start(f32[12,4,128]{2,0,1:T(8,128)S(1)} %copy.38), channel_id=1, source_target_pairs={{1,0},{2,1},{3,2},{4,3},{5,4},{6,5},{7,6},{8,7},{9,8},{10,9},{11,1... | collective-permute-start | bytes 73736 | tf_op jit(solution)/shard_map/ppermute | solution.py:21
  17.9 9.3 %collective-permute-start.2 = (f32[13,4,128]{2,0,1:T(8,128)S(1)}, f32[13,4,128]{2,0,1:T(8,128)S(1)}, u32[]{:S(2)}, u32[]{:S(2)}) collective-permute-start(f32[13,4,128]{2,0,1:T(8,128)S(1)} %get-tuple-element.148), channel_id=1, source_target_pairs={{0,1},{1,2},{2,3},{3,4},{4,5},{5,6},{6,7},{7,8},{8,9},{9,10},{10,1... | collective-permute-start | bytes 79880 | tf_op jit(solution)/shard_map/ppermute | solution.py:20
  19.9 7.9 %collective-permute-start.3 = (f32[13,4,128]{2,0,1:T(8,128)S(1)}, f32[13,4,128]{2,0,1:T(8,128)S(1)}, u32[]{:S(2)}, u32[]{:S(2)}) collective-permute-start(f32[13,4,128]{2,0,1:T(8,128)S(1)} %get-tuple-element.149), channel_id=1, source_target_pairs={{1,0},{2,1},{3,2},{4,3},{5,4},{6,5},{7,6},{8,7},{9,8},{10,9},{11,1... | collective-permute-start | bytes 79880 | tf_op jit(solution)/shard_map/ppermute | solution.py:21
  30.2 19.2 %copy-start = (s32[2,4096]{1,0:T(2,128)S(1)}, s32[2,4096]{1,0:T(2,128)}, u32[]{:S(2)}) copy-start(s32[2,4096]{1,0:T(2,128)} %param.14) | copy-start | bytes 98308
  31.6 33.5 %all-to-all-start = ((f32[12,16,128]{2,0,1:T(8,128)}), f32[12,16,128]{2,0,1:T(8,128)S(1)}, u32[]{:S(2)}, u32[]{:S(2)}) async-start(f32[12,16,128]{2,0,1:T(8,128)} %slice_add_fusion.8), calls=%async_computation | async-start | bytes 262144 | tf_op jit(solution)/shard_map/all_to_all | solution.py:114
  49.3 530.8 %all-reduce.21.cloned.1.call-start = ((), (), s32[]{:S(2)}) async-start(), calls=%async_computation.2 | async-start | bytes 8388608 | tf_op jit(solution)/shard_map/psum | solution.py:146
  93.3 0.7 copy-start.1
  93.3 0.7 copy-start.2
  94.1 492.2 %copy-start.3 = (f32[1024]{0:T(1024)S(1)}, f32[1024]{0:T(1024)}, u32[]{:S(2)}) copy-start(f32[1024]{0:T(1024)} %param.16) | copy-start | bytes 12292
  643.1 26.8 %all-to-all-start.1 = ((f32[192,1,128]{2,1,0:T(1,128)}), f32[192,1,128]{2,1,0:T(1,128)S(1)}, u32[]{:S(2)}, u32[]{:S(2)}) async-start(f32[192,1,128]{2,1,0:T(1,128)} %bitcast.21), calls=%async_computation.1 | async-start | bytes 196608 | tf_op jit(solution)/shard_map/all_to_all | solution.py:153
Sparse Core Ops, SparseCore 0:
  93.5 486.5 all-reduce.20
where the time goes:
time: 678 us; the launch traced here: 677 us
  waiting for transfers between devices  515 us (76%)
  other arithmetic  55.2 us (8%)
  starting transfers between devices  45.8 us (7%)
  local copies, waits for them, and re-layouts  19.3 us (3%)
  between operations  15.8 us (2%)
  loops' own time  13.8 us (2%)
  matrix products  12.1 us (2%)
    psum x1, waiting for transfers between devices, shards(): lax.psum(lax.map(pixel_block, offsets).reshape(pixel_total, sample_vector...  486 us
    another operation x7, other arithmetic, finish(): factor = jnp.linalg.cholesky(gram)  28.7 us
    another operation x6, other arithmetic, finish(): inverse = jax.scipy.linalg.solve_triangular(factor, ident, lower=True)  20 us
    all_to_all x1, starting transfers between devices, shards(): lax.all_to_all(predicted_ensemble, 'member', split_axis=1, concat_axis=0,...  17.7 us
    all_to_all x1, waiting for transfers between devices, shards(): lax.all_to_all(predicted_ensemble, 'member', split_axis=1, concat_axis=0,...  15 us
    all_to_all x1, waiting for transfers between devices, shards(): lax.all_to_all(analysed, 'member', split_axis=0, concat_axis=1, tiled=True)  13.9 us
    another operation x1, loops' own time, shards(): lax.map(pixel_block, offsets).reshape(pixel_total, sample_vectors)  13.8 us
  transfers between devices with their start and end apart: 7, of which 4 were waited for; matrix products, arithmetic and copies ran while one was open for 1% of the time, Pallas kernels for 0%

commit v1 on v0

--- a/solution.py
+++ b/solution.py
@@ -144,7 +144,8 @@
 
     offsets = 0 + block * jnp.arange(pixel_total // block, dtype=jnp.int32)
     whole = lax.psum(
-        lax.map(pixel_block, offsets).reshape(pixel_total, sample_vectors), ("member", "slab")
+        lax.psum(lax.map(pixel_block, offsets).reshape(pixel_total, sample_vectors), "member"),
+        "slab",
     )
     own_part = lax.dynamic_slice_in_dim(whole, own_first, own_rows, 0)
     predicted = jnp.take(whole, obs_index, axis=0)

time: 678 us -> 889 us (1.31)
  the two profiles are of different devices: /device:TPU:8 before, /device:TPU:2 now
where the time goes in v1:
time: 889 us; the launch traced here: 888 us
  waiting for transfers between devices  732 us (82%)
  other arithmetic  55.2 us (6%)
  starting transfers between devices  40.6 us (5%)
  local copies, waits for them, and re-layouts  18.5 us (2%)
  between operations  15.8 us (2%)
  loops' own time  13.8 us (2%)
  matrix products  12.1 us (1%)
    psum x1, waiting for transfers between devices, shards(): lax.psum(lax.map(pixel_block, offsets).reshape(pixel_total, sample_vector...  399 us
    psum x1, waiting for transfers between devices, shards(): lax.psum(lax.psum(lax.map(pixel_block, offsets).reshape(pixel_total, samp...  304 us
    another operation x7, other arithmetic, finish(): factor = jnp.linalg.cholesky(gram)  28.7 us
    another operation x6, other arithmetic, finish(): inverse = jax.scipy.linalg.solve_triangular(factor, ident, lower=True)  20 us
  transfers between devices with their start and end apart: 8, of which 5 were waited for; matrix products, arithmetic and copies ran while one was open for 1% of the time, Pallas kernels for 0%

profile of v1, /device:TPU:2, one launch (start us, length us, event | category | flops | bytes accessed | tf_op | source)
XLA Modules:
  0.0 888.4 jit_solution(936272523450704151)
XLA Ops:
  8.0 1.7 collective-permute-start
  9.8 1.3 collective-permute-start.1
  11.1 0.9 copy.28
  12.7 4.7 collective-permute-start.2
  17.5 1.3 collective-permute-start.3
  18.8 0.9 copy_dynamic-update-slice_fusion
  19.8 2.0 collective-permute-done.3
  25.6 17.2 %all-to-all-start = ((f32[12,16,128]{2,0,1:T(8,128)}), f32[12,16,128]{2,0,1:T(8,128)S(1)}, u32[]{:S(2)}, u32[]{:S(2)}) async-start(f32[12,16,128]{2,0,1:T(8,128)} %slice_add_fusion.8), calls=%async_computation | async-start | bytes 262144 | tf_op jit(solution)/shard_map/all_to_all | solution.py:114
  43.7 15.5 %all-to-all-done = f32[12,16,128]{2,0,1:T(8,128)S(1)} async-done(((f32[12,16,128]{2,0,1:T(8,128)}), f32[12,16,128]{2,0,1:T(8,128)S(1)}, u32[]{:S(2)}, u32[]{:S(2)}) %all-to-all-start) | async-done | bytes 98336 | tf_op jit(solution)/shard_map/all_to_all | solution.py:114
  59.1 24.8 %while.14 = (s32[]{:T(128)}, f32[8,512,192]{1,2,0:T(8,128)S(1)}, f32[1,128]{1,0:T(1,128)S(1)}, f32[1,1]{1,0:T(1,128)}, s32[8]{0:T(128)S(1)}, /*index=5*/f32[2,40...) while((s32[]{:T(128)}, f32[8,512,192]{1,2,0:T(8,128)S(1)}, ...), condition=%wide.region_2.3_spmd.clone, body=%wide.region_1.2_spmd.clone.sunk | while | flops 151389696 | bytes 507079 | solution.py:147
  83.9 3.4 copy.29
  87.6 398.7 %all-reduce.22.cloned.1.call-done = f32[4096,192]{1,0:T(8,128)} async-done(((f32[4096,192]{1,0:T(8,128)}), f32[4096,192]{1,0:T(8,128)}) %all-reduce.22.cloned.1.call-update) | async-done | bytes 3145744 | tf_op jit(solution)/shard_map/psum | solution.py:147
  486.5 303.9 %all-reduce.24.cloned.1.call-done = f32[4096,192]{1,0:T(8,128)} async-done(((f32[4096,192]{1,0:T(8,128)}), f32[4096,192]{1,0:T(8,128)}) %all-reduce.24.cloned.1.call-update) | async-done | bytes 3145744 | tf_op jit(solution)/shard_map/psum | solution.py:146
  790.5 5.6 gather_fusion
  796.5 2.5 fusion.17
  799.2 11.7 %cholesky.50 = f32[128,128]{1,0:T(8,128)S(1)} custom-call(f32[128,128]{1,0:T(8,128)S(1)} %cholesky.121), custom_call_target="Cholesky" | custom-call | tf_op jit(solution)/shard_map/jit(cholesky)/cholesky | solution.py:65
  811.0 0.9 fusion.19
  812.5 9.8 %custom-call.15 = f32[1,128,128]{1,2,0:T(8,128)S(1)} custom-call(f32[1,128,128]{2,1,0:T(8,128)S(1)} %get-tuple-element.153), custom_call_target="InvertDiagBlocksLowerTriangular" | custom-call | tf_op jit(solution)/shard_map/jit(cholesky)/cholesky | solution.py:65
  822.7 5.8 cholesky.108
  830.7 19.9 %custom-call.16 = f32[2,128,128]{1,2,0:T(8,128)S(1)} custom-call(f32[2,128,128]{2,1,0:T(8,128)S(1)} %pad_maximum_fusion.2), custom_call_target="InvertDiagBlocksLowerTriangular" | custom-call | tf_op jit(solution)/shard_map/jit(_solve_triangular)/triangular_solve | solution.py:66
  852.0 1.3 convolution_add_fusion
  853.3 14.1 %all-to-all-start.1 = ((f32[192,1,128]{2,1,0:T(1,128)}), f32[192,1,128]{2,1,0:T(1,128)S(1)}, u32[]{:S(2)}, u32[]{:S(2)}) async-start(f32[192,1,128]{2,1,0:T(1,128)} %bitcast.21), calls=%async_computation.1 | async-start | bytes 196608 | tf_op jit(solution)/shard_map/all_to_all | solution.py:154
  867.4 1.3 constant_dynamic-slice_fusion
  868.7 12.2 %all-to-all-done.1 = f32[192,1,128]{2,1,0:T(1,128)S(1)} async-done(((f32[192,1,128]{2,1,0:T(1,128)}), f32[192,1,128]{2,1,0:T(1,128)S(1)}, u32[]{:S(2)}, u32[]{:S(2)}) %all-to-all-start.1) | async-done | bytes 98336 | tf_op jit(solution)/shard_map/all_to_all | solution.py:154
  (113 shorter events, 21.9 us)
Async XLA Ops:
  8.0 10.8 %collective-permute-start = (f32[12,4,128]{2,0,1:T(8,128)S(1)}, f32[12,4,128]{2,0,1:T(8,128)S(1)}, u32[]{:S(2)}, u32[]{:S(2)}) collective-permute-start(f32[12,4,128]{2,0,1:T(8,128)S(1)} %copy.37), channel_id=1, source_target_pairs={{0,1},{1,2},{2,3},{3,4},{4,5},{5,6},{6,7},{7,8},{8,9},{9,10},{10,1... | collective-permute-start | bytes 73736 | tf_op jit(solution)/shard_map/ppermute | solution.py:20
  9.8 10.0 %collective-permute-start.1 = (f32[12,4,128]{2,0,1:T(8,128)S(1)}, f32[12,4,128]{2,0,1:T(8,128)S(1)}, u32[]{:S(2)}, u32[]{:S(2)}) collective-permute-start(f32[12,4,128]{2,0,1:T(8,128)S(1)} %copy.38), channel_id=1, source_target_pairs={{1,0},{2,1},{3,2},{4,3},{5,4},{6,5},{7,6},{8,7},{9,8},{10,9},{11,1... | collective-permute-start | bytes 73736 | tf_op jit(solution)/shard_map/ppermute | solution.py:21
  12.7 7.0 collective-permute-start.2
  17.5 4.3 collective-permute-start.3
  24.2 18.7 %copy-start = (s32[2,4096]{1,0:T(2,128)S(1)}, s32[2,4096]{1,0:T(2,128)}, u32[]{:S(2)}) copy-start(s32[2,4096]{1,0:T(2,128)} %param.14) | copy-start | bytes 98308
  25.6 33.5 %all-to-all-start = ((f32[12,16,128]{2,0,1:T(8,128)}), f32[12,16,128]{2,0,1:T(8,128)S(1)}, u32[]{:S(2)}, u32[]{:S(2)}) async-start(f32[12,16,128]{2,0,1:T(8,128)} %slice_add_fusion.8), calls=%async_computation | async-start | bytes 262144 | tf_op jit(solution)/shard_map/all_to_all | solution.py:114
  42.8 443.5 %all-reduce.22.cloned.1.call-start = ((), (), s32[]{:S(2)}) async-start(), calls=%async_computation.2 | async-start | bytes 8388608 | tf_op jit(solution)/shard_map/psum | solution.py:147
  87.3 399.1 %copy-start.1 = (s32[1024]{0:T(1024)S(1)}, s32[1024]{0:T(1024)}, u32[]{:S(2)}) copy-start(s32[1024]{0:T(1024)} %param.15) | copy-start | bytes 12292
  87.4 399.1 %copy-start.2 = (f32[1024]{0:T(1024)S(1)}, f32[1024]{0:T(1024)}, u32[]{:S(2)}) copy-start(f32[1024]{0:T(1024)} %param.17) | copy-start | bytes 12292
  87.4 703.1 %all-reduce.24.cloned.1.call-start = ((), (), s32[]{:S(2)}) async-start(), calls=%async_computation.3 | async-start | bytes 8388608 | tf_op jit(solution)/shard_map/psum | solution.py:146
  486.5 310.0 %copy-start.3 = (f32[1024]{0:T(1024)S(1)}, f32[1024]{0:T(1024)}, u32[]{:S(2)}) copy-start(f32[1024]{0:T(1024)} %param.16) | copy-start | bytes 12292
  853.3 27.6 %all-to-all-start.1 = ((f32[192,1,128]{2,1,0:T(1,128)}), f32[192,1,128]{2,1,0:T(1,128)S(1)}, u32[]{:S(2)}, u32[]{:S(2)}) async-start(f32[192,1,128]{2,1,0:T(1,128)} %bitcast.21), calls=%async_computation.1 | async-start | bytes 196608 | tf_op jit(solution)/shard_map/all_to_all | solution.py:154
Sparse Core Ops, SparseCore 0:
  87.5 398.7 all-reduce.21
  489.2 301.1 all-reduce.23
